TPU v7x, 256 devices: a whole 4x4x8 slice. The times are simulated.
256 devices in a mesh: cube: 16 (over z, x_hi), row: 4 (over x_lo, core), col: 4 (over y).
Axes of the slice: x: 4 (x_hi: 2, x_lo: 2; x = x_hi * 2 + x_lo), y: 4, z: 8, core: 2. Of those that a mesh axis runs over, the one named last changes fastest.
Arguments:
- diag_block: float32 [16, 512, 512], P('cube'), as said below
- panel: float32 [16, 8192, 512], P('cube', ('row', 'col')), may hold values from -2.4 to 2.4
- trailing: float32 [16, 2048, 8192], P('cube', 'col', 'row'), may hold values from -6 to 6
- parent_front: float32 [16, 512, 8192], P('cube', 'col', 'row'), may hold values from -6 to 6
- front_order: int32 [16], P('cube'), may hold values from 4096 to 8192, as said below
- dest_group: int32 [16, 4, 4, 64, 1], P(None, 'col', 'row'), may hold values from 0 to 15; in each aligned block of 64 rows (0 to 63, 64 to 127, ..., all dimensions but the last counted through in order) at most 8 rows name the same one
- parent_block: int32 [16, 4, 4, 64, 1], P(None, 'col', 'row'), may hold values from 0 to 15
Outputs:
- assembled: float32 [16, 512, 8192], P('cube', 'col', 'row')
Inputs may be any that keep to these rules, and one draw needn't show every extreme that they name: `front_order`: a multiple of 128; each group's update matrix is zero in the columns at or beyond it. `dest_group`: at most 8 of the 64 blocks of one device and group go to one group. `diag_block`: symmetric positive definite.
All inputs are finite; a program needn't handle non-finite values.
Results may differ from a plain program's by a relative error of at most 0.0003.
Values sent between devices are 32-bit elements; how exact they have to be, the bound alone decides.
A program may use at most 128 MiB of HBM per device.

v0:
```python
import jax
import jax.numpy as jnp
from jax import lax
from jax.sharding import PartitionSpec as P

BS = 128


def spread(value, axis, root):
    mine = lax.axis_index(axis) == root
    return lax.psum(jnp.where(mine, value, jnp.zeros_like(value)), axis)


def shards(diag_block, panel, trailing, parent_front, front_order, dest_group, parent_block):
    precise_mode = lax.Precision.HIGHEST
    chol_diag = jnp.linalg.cholesky(diag_block[0])
    panel_factor = lax.linalg.triangular_solve(
        chol_diag, panel[0], left_side=False, lower=True, transpose_a=True
    )
    slab_factor = spread(panel_factor, "row", 0)
    product = lax.dot_general(
        slab_factor,
        lax.all_gather(panel_factor, "col", axis=0, tiled=True),
        (((1,), (1,)), ((), ())),
        precision=precise_mode,
    )
    device_rows = trailing.shape[1]
    cols_dev = trailing.shape[2]
    column_ids = lax.axis_index("row") * cols_dev + jnp.arange(cols_dev, dtype=jnp.int32)
    update = jnp.where(
        column_ids[None, :] < front_order[0], trailing[0] - product, jnp.float32(0.0)
    )
    block_rows = device_rows // BS
    block_cols = cols_dev // BS
    blocks = (
        update.reshape(block_rows, BS, block_cols, BS)
        .transpose(0, 2, 1, 3)
        .reshape(block_rows * block_cols, BS * BS)
    )
    nblocks = block_rows * block_cols
    groups = lax.axis_size("cube")
    own_group = lax.axis_index("cube")
    dest_all = dest_group[:, 0, 0, :, 0]
    parent_all = parent_block[:, 0, 0, :, 0]
    dest_mine = lax.dynamic_index_in_dim(dest_all, own_group, 0, keepdims=False)
    parent_rows = parent_front.shape[1]
    parent_brows = parent_rows // BS
    nparent = parent_brows * block_cols
    capacity = 2 * nblocks // groups
    hit_table = (dest_mine[:, None] == jnp.arange(groups, dtype=jnp.int32)[None, :]).astype(
        jnp.int32
    )
    before = jnp.cumsum(hit_table, axis=0) - hit_table
    slot_ids = jnp.sum(before * hit_table, axis=1)
    position = dest_mine * capacity + slot_ids
    picker = (position[None, :] == jnp.arange(groups * capacity, dtype=jnp.int32)[:, None]).astype(
        jnp.float32
    )
    outgoing = jnp.dot(picker, blocks, precision=precise_mode).reshape(groups, capacity, BS * BS)
    incoming = lax.all_to_all(outgoing, "cube", split_axis=0, concat_axis=0, tiled=True)
    arriving = (dest_all == own_group).astype(jnp.int32)
    rank_ids = jnp.cumsum(arriving, axis=1) - arriving
    in_slot = (
        arriving[:, :, None]
        * (rank_ids[:, :, None] == jnp.arange(capacity, dtype=jnp.int32)[None, None, :])
    ).astype(jnp.float32)
    to_parent = (
        parent_all[:, :, None] == jnp.arange(nparent, dtype=jnp.int32)[None, None, :]
    ).astype(jnp.float32)
    weight = jnp.einsum("sbk,sbp->psk", in_slot, to_parent, precision=precise_mode)
    assembled = jnp.dot(
        weight.reshape(nparent, groups * capacity),
        incoming.reshape(groups * capacity, BS * BS),
        precision=precise_mode,
    )
    assembled = (
        assembled.reshape(parent_brows, block_cols, BS, BS)
        .transpose(0, 2, 1, 3)
        .reshape(parent_rows, cols_dev)
    )
    return (parent_front[0] + assembled)[None]


def solution(mesh):
    placed = (
        P("cube", None, None),
        P("cube", ("row", "col"), None),
        P("cube", "col", "row"),
        P("cube", "col", "row"),
        P("cube"),
        P(None, "col", "row", None, None),
        P(None, "col", "row", None, None),
    )
    return jax.shard_map(
        shards, mesh=mesh, in_specs=placed, out_specs=P("cube", "col", "row"), check_vma=False
    )
```

profile of v0, /device:TPU:1, one launch (start us, length us, event | category | flops | bytes accessed | tf_op | source)
XLA Modules:
  0.0 464.2 jit_solution(15554430962399069206)
XLA Ops:
  7.4 1.6 copy.9
  10.4 11.7 %cholesky.104 = f32[128,128]{1,0:T(8,128)S(1)} custom-call(f32[128,128]{1,0:T(8,128)S(1)} %cholesky.266), custom_call_target="Cholesky" | custom-call | tf_op jit(solution)/shard_map/jit(cholesky)/cholesky | solution.py:16
  22.2 9.8 %custom-call.30 = f32[1,128,128]{1,2,0:T(8,128)S(1)} custom-call(f32[1,128,128]{2,1,0:T(8,128)S(1)} %get-tuple-element.34), custom_call_target="InvertDiagBlocksLowerTriangular" | custom-call | tf_op jit(solution)/shard_map/jit(cholesky)/cholesky | solution.py:16
  32.8 11.7 %cholesky.217 = f32[128,128]{1,0:T(8,128)S(1)} custom-call(f32[128,128]{1,0:T(8,128)S(1)} %cholesky.270), custom_call_target="Cholesky" | custom-call | tf_op jit(solution)/shard_map/jit(cholesky)/cholesky | solution.py:16
  44.5 10.0 %custom-call.31 = f32[1,128,128]{1,2,0:T(8,128)S(1)} custom-call(f32[1,128,128]{2,1,0:T(8,128)S(1)} %get-tuple-element.31), custom_call_target="InvertDiagBlocksLowerTriangular" | custom-call | tf_op jit(solution)/shard_map/jit(cholesky)/cholesky | solution.py:16
  55.2 11.7 %cholesky.238 = f32[128,128]{1,0:T(8,128)S(1)} custom-call(f32[128,128]{1,0:T(8,128)S(1)} %cholesky.275), custom_call_target="Cholesky" | custom-call | tf_op jit(solution)/shard_map/jit(cholesky)/cholesky | solution.py:16
  67.5 9.8 %custom-call.32 = f32[1,128,128]{1,2,0:T(8,128)S(1)} custom-call(f32[1,128,128]{2,1,0:T(8,128)S(1)} %get-tuple-element.28), custom_call_target="InvertDiagBlocksLowerTriangular" | custom-call | tf_op jit(solution)/shard_map/jit(cholesky)/cholesky | solution.py:16
  78.0 11.7 %cholesky.255 = f32[128,128]{1,0:T(8,128)S(1)} custom-call(f32[128,128]{1,0:T(8,128)S(1)} %convolution_subtract_fusion.5), custom_call_target="Cholesky" | custom-call | tf_op jit(solution)/shard_map/jit(cholesky)/cholesky | solution.py:16
  93.9 10.1 %while.1 = (s32[]{:T(128)}, f32[512,512]{1,0:T(8,128)S(1)}, s32[4,2]{0,1:T(2,128)S(1)}, f32[4,128,128]{2,1,0:T(8,128)}, s32[]{:T(128)}) while((s32[]{:T(128)}, f32[512,512]{1,0:T(8,128)S(1)}, s32[4,2]{0,1:T(2,128)S(1)}, f32[4,128,128]{2,1,0:T(8,128)}, s32[]{:T(128)}) %tuple.28), condition=%wide.while_cond, body=%wide.while_body.sunk | while | flops 2 | bytes 132705 | solution.py:17
  94.5 1.9 bitcast_dynamic-update-slice_fusion.2
  97.0 1.9 bitcast_dynamic-update-slice_fusion.2
  99.6 1.9 bitcast_dynamic-update-slice_fusion.2
  102.1 1.9 bitcast_dynamic-update-slice_fusion.2
  104.0 40.1 %custom-call.33 = f32[4,128,128]{1,2,0:T(8,128)S(1)} custom-call(f32[4,128,128]{2,1,0:T(8,128)} %get-tuple-element.12), custom_call_target="InvertDiagBlocksLowerTriangular" | custom-call | tf_op jit(solution)/shard_map/triangular_solve | solution.py:17
  151.0 49.6 %all-reduce.3.cloned.1.call-done = f32[512,512]{1,0:T(8,128)} async-done(((f32[512,512]{1,0:T(8,128)}), f32[512,512]{1,0:T(8,128)}) %all-reduce.3.cloned.1.call-update) | async-done | bytes 1048592 | tf_op jit(solution)/shard_map/psum | solution.py:11
  200.6 5.6 %all-gather.2.cloned.1.call-done = f32[2048,512]{1,0:T(8,128)} async-done(((f32[512,512]{1,0:T(8,128)}), f32[2048,512]{1,0:T(8,128)}) %all-gather.2.cloned.1.call-update) | async-done | bytes 4194320 | tf_op jit(solution)/shard_map/all_gather | solution.py:23
  206.2 9.7 %fusion.1 = f32[64,8,16,128]{3,1,2,0:T(8,128)S(1)} fusion(f32[1,512,2048]{2,1,0:T(8,128)} %param.9, f32[512,512]{1,0:T(8,128)} %all-reduce.3.cloned.1.call-done, f32[2048,512]{1,0:T(8,128)} %all-gather.2.cloned.1.call-done, pred[2048]{0:T(1024)(128)(4,1)S(1)} %add_compare_fusion), kind=kOutput, calls=%fused_computation.5 | convolution fusion | flops 6444548096 | bytes 13633536 | tf_op jit(solution)/shard_map/dot_general | solution.py:21
  217.2 3.3 copy.18
  220.4 4.9 %reshape.146 = f32[64,16384,1]{1,0,2:T(8,128)} reshape(f32[4,16,128,128]{3,2,1,0:T(8,128)} %copy.18) | data formatting | bytes 8388608 | tf_op jit(solution)/shard_map/reshape | solution.py:38
  225.4 8.7 %fusion.33 = f32[16,8,16384]{2,1,0:T(8,128)} fusion(f32[64,16384,1]{1,0,2:T(8,128)} %reshape.146, s32[16,8]{1,0:T(8,128)S(1)} %multiply_add_fusion, s32[64]{0:T(128)S(1)} %multiply_add_fusion.1), kind=kOutput, calls=%fused_computation.67 | convolution fusion | flops 1610620928 | bytes 12583680 | tf_op jit(solution)/shard_map/dot_general | solution.py:59
  234.1 9.7 %all-to-all-start = ((f32[16,8,16384]{2,1,0:T(8,128)}), f32[16,8,16384]{2,1,0:T(8,128)}, u32[]{:S(2)}, u32[]{:S(2)}) async-start(f32[16,8,16384]{2,1,0:T(8,128)} %fusion.33), calls=%async_computation | async-start | bytes 16777216 | tf_op jit(solution)/shard_map/all_to_all | solution.py:60
  244.3 192.4 %all-to-all-done = f32[16,8,16384]{2,1,0:T(8,128)} async-done(((f32[16,8,16384]{2,1,0:T(8,128)}), f32[16,8,16384]{2,1,0:T(8,128)}, u32[]{:S(2)}, u32[]{:S(2)}) %all-to-all-start) | async-done | bytes 8388640 | tf_op jit(solution)/shard_map/all_to_all | solution.py:60
  436.7 9.0 %copy.19 = f32[16384,128]{1,0:T(8,128)} copy(f32[16384,128]{0,1:T(8,128)} %bitcast.26) | data formatting | bytes 16777216 | tf_op jit(solution)/shard_map/dot_general | solution.py:71
  445.7 9.4 %convolution_bitcast_fusion = f32[1,128,16,128]{3,2,1,0:T(8,128)S(1)} fusion(f32[16,128,1]{0,1,2:T(8,128)S(1)} %convolution_bitcast_fusion.1, f32[128,128,128]{2,1,0:T(8,128)} %bitcast.103), kind=kOutput, calls=%fused_computation.6 | convolution fusion | flops 402653184 | bytes 9445376 | tf_op jit(solution)/shard_map/dot_general | solution.py:71
  (66 shorter events, 17.3 us)
Async XLA Ops:
  7.4 193.2 %all-reduce.3.cloned.1.call-start = ((), (), s32[]{:S(2)}) async-start(), calls=%async_computation.1 | async-start | bytes 2097152 | tf_op jit(solution)/shard_map/psum | solution.py:11
  10.4 133.8 %copy-start.1 = (f32[1,512,512]{2,1,0:T(8,128)S(1)}, f32[1,512,512]{2,1,0:T(8,128)}, u32[]{:S(2)}) copy-start(f32[1,512,512]{2,1,0:T(8,128)} %param.8) | copy-start | bytes 3145732
  146.3 4.3 copy-start.2
  149.4 56.8 %all-gather.2.cloned.1.call-start = ((), (), s32[]{:S(2)}) async-start(), calls=%async_computation.2 | async-start | bytes 5242880 | tf_op jit(solution)/shard_map/all_gather | solution.py:23
  234.1 10.0 %copy-start.3 = (s32[16,1,1,64,1]{3,4,2,1,0:T(1,128)S(1)}, s32[16,1,1,64,1]{3,4,2,1,0:T(1,128)}, u32[]{:S(2)}) copy-start(s32[16,1,1,64,1]{3,4,2,1,0:T(1,128)} %param.13) | copy-start | bytes 12292
  234.1 202.6 %all-to-all-start = ((f32[16,8,16384]{2,1,0:T(8,128)}), f32[16,8,16384]{2,1,0:T(8,128)}, u32[]{:S(2)}, u32[]{:S(2)}) async-start(f32[16,8,16384]{2,1,0:T(8,128)} %fusion.33), calls=%async_computation | async-start | bytes 16777216 | tf_op jit(solution)/shard_map/all_to_all | solution.py:60
  445.7 9.6 %copy-start = (f32[1,128,2048]{2,1,0:T(8,128)S(1)}, f32[1,128,2048]{2,1,0:T(8,128)}, u32[]{:S(2)}) copy-start(f32[1,128,2048]{2,1,0:T(8,128)} %param.10) | copy-start | bytes 3145732
Sparse Core Ops, SparseCore 0:
  149.5 51.0 all-reduce.2
Sparse Core Ops, SparseCore 1:
  151.8 54.4 all-gather.1
where the time goes:
time: 473 us; the launch traced here: 464 us
  waiting for transfers between devices  248 us (52%)
  other arithmetic  123 us (26%)
  matrix products  33.4 us (7%)
  local copies, waits for them, and re-layouts  30.6 us (6%)
  between operations  18.9 us (4%)
  starting transfers between devices  9.75 us (2%)
    all_to_all x1, waiting for transfers between devices, shards(): lax.all_to_all(outgoing, 'cube', split_axis=0, concat_axis=0, tiled=True)  192 us
    another operation x14, other arithmetic, shards(): chol_diag = jnp.linalg.cholesky(diag_block[0])  78.6 us
    psum x1, waiting for transfers between devices, spread(): return lax.psum(jnp.where(mine, value, jnp.zeros_like(value)), axis)  49.6 us
    another operation x4, other arithmetic, shards(): lax.linalg.triangular_solve(chol_diag, panel[0], left_side=False, lower=T...  41.8 us
    another operation x12, local copies, waits for them, and re-layouts  10.1 us
    all_to_all x1, starting transfers between devices, shards(): lax.all_to_all(outgoing, 'cube', split_axis=0, concat_axis=0, tiled=True)  9.7 us
    dot_general x1, matrix products, shards(): lax.dot_general(slab_factor, lax.all_gather(panel_factor, 'col', axis=0,...  9.67 us
  transfers between devices with their start and end apart: 3, of which 3 were waited for; matrix products, arithmetic and copies ran while one was open for 0% of the time, Pallas kernels for 0%

commit v1 on v0

--- a/solution.py
+++ b/solution.py
@@ -6,9 +6,15 @@
 BS = 128
 
 
+def summed_here(array, name):
+    parts = lax.all_gather(array, name, axis=0, tiled=False)
+    result = parts.sum(axis=0)
+    return result
+
+
 def spread(value, axis, root):
     mine = lax.axis_index(axis) == root
-    return lax.psum(jnp.where(mine, value, jnp.zeros_like(value)), axis)
+    return summed_here(jnp.where(mine, value, jnp.zeros_like(value)), axis)
 
 
 def shards(diag_block, panel, trailing, parent_front, front_order, dest_group, parent_block):

time: 473 us -> 524 us (1.11)
  waiting for transfers between devices: 248 us -> 294 us
    all_gather x0 -> x1, waiting for transfers between devices: none -> 51.2 us  [summed_here(): parts = lax.all_gather(array, name, axis=0, tiled=False)]
    psum x1 -> x0, waiting for transfers between devices: 49.6 us -> none  [spread(): return lax.psum(jnp.where(mine, value, jnp.zeros_like(value)), axis)]
    all_gather x1, waiting for transfers between devices: 5.58 us -> 50.3 us  [shards(): lax.all_gather(panel_factor, 'col', axis=0, tiled=True)]
  transfers between devices with their start and end apart: 3 -> 3, of which waited for: 3 -> 3; matrix products, arithmetic and copies ran while one was open for 0% -> 1% of each run, Pallas kernels for 0% -> 0%
where the time goes in v1:
time: 524 us; the launch traced here: 515 us
  waiting for transfers between devices  294 us (56%)
  other arithmetic  125 us (24%)
  matrix products  38.3 us (7%)
  local copies, waits for them, and re-layouts  29.7 us (6%)
  between operations  17.4 us (3%)
  starting transfers between devices  9.78 us (2%)
    all_to_all x1, waiting for transfers between devices, shards(): lax.all_to_all(outgoing, 'cube', split_axis=0, concat_axis=0, tiled=True)  192 us
    another operation x14, other arithmetic, shards(): chol_diag = jnp.linalg.cholesky(diag_block[0])  78.6 us
    all_gather x1, waiting for transfers between devices, summed_here(): parts = lax.all_gather(array, name, axis=0, tiled=False)  51.2 us
    all_gather x1, waiting for transfers between devices, shards(): lax.all_gather(panel_factor, 'col', axis=0, tiled=True)  50.3 us
    another operation x4, other arithmetic, shards(): lax.linalg.triangular_solve(chol_diag, panel[0], left_side=False, lower=T...  40.6 us
  transfers between devices with their start and end apart: 3, of which 3 were waited for; matrix products, arithmetic and copies ran while one was open for 1% of the time, Pallas kernels for 0%

profile of v1, /device:TPU:1, one launch (start us, length us, event | category | flops | bytes accessed | tf_op | source)
XLA Modules:
  0.0 514.7 jit_solution(18135571491551536149)
XLA Ops:
  6.5 1.6 copy.15
  9.6 11.7 %cholesky.105 = f32[128,128]{1,0:T(8,128)S(1)} custom-call(f32[128,128]{1,0:T(8,128)S(1)} %cholesky.269), custom_call_target="Cholesky" | custom-call | tf_op jit(solution)/shard_map/jit(cholesky)/cholesky | solution.py:22
  21.3 9.8 %custom-call.30 = f32[1,128,128]{1,2,0:T(8,128)S(1)} custom-call(f32[1,128,128]{2,1,0:T(8,128)S(1)} %get-tuple-element.32), custom_call_target="InvertDiagBlocksLowerTriangular" | custom-call | tf_op jit(solution)/shard_map/jit(cholesky)/cholesky | solution.py:22
  31.9 11.7 %cholesky.219 = f32[128,128]{1,0:T(8,128)S(1)} custom-call(f32[128,128]{1,0:T(8,128)S(1)} %cholesky.273), custom_call_target="Cholesky" | custom-call | tf_op jit(solution)/shard_map/jit(cholesky)/cholesky | solution.py:22
  43.7 10.0 %custom-call.31 = f32[1,128,128]{1,2,0:T(8,128)S(1)} custom-call(f32[1,128,128]{2,1,0:T(8,128)S(1)} %get-tuple-element.29), custom_call_target="InvertDiagBlocksLowerTriangular" | custom-call | tf_op jit(solution)/shard_map/jit(cholesky)/cholesky | solution.py:22
  54.3 11.7 %cholesky.240 = f32[128,128]{1,0:T(8,128)S(1)} custom-call(f32[128,128]{1,0:T(8,128)S(1)} %cholesky.278), custom_call_target="Cholesky" | custom-call | tf_op jit(solution)/shard_map/jit(cholesky)/cholesky | solution.py:22
  66.8 9.8 %custom-call.32 = f32[1,128,128]{1,2,0:T(8,128)S(1)} custom-call(f32[1,128,128]{2,1,0:T(8,128)S(1)} %get-tuple-element.26), custom_call_target="InvertDiagBlocksLowerTriangular" | custom-call | tf_op jit(solution)/shard_map/jit(cholesky)/cholesky | solution.py:22
  77.2 11.7 %cholesky.257 = f32[128,128]{1,0:T(8,128)S(1)} custom-call(f32[128,128]{1,0:T(8,128)S(1)} %convolution_subtract_fusion.5), custom_call_target="Cholesky" | custom-call | tf_op jit(solution)/shard_map/jit(cholesky)/cholesky | solution.py:22
  92.9 8.4 %while.1 = (s32[]{:T(128)}, f32[512,512]{1,0:T(8,128)S(1)}, s32[4,2]{0,1:T(2,128)S(1)}, f32[4,128,128]{2,1,0:T(8,128)S(1)}, s32[]{:T(128)}) while((s32[]{:T(128)}, f32[512,512]{1,0:T(8,128)S(1)}, s32[4,2]{0,1:T(2,128)S(1)}, f32[4,128,128]{2,1,0:T(8,128)S(1)}, s32[]{:T(128)}) %tuple.27), condition=%wide.while_cond, body=%wide.while_body.sunk | while | flops 2 | bytes 131181 | solution.py:23
  101.3 39.3 %custom-call.33 = f32[4,128,128]{1,2,0:T(8,128)S(1)} custom-call(f32[4,128,128]{2,1,0:T(8,128)S(1)} %get-tuple-element.12), custom_call_target="InvertDiagBlocksLowerTriangular" | custom-call | tf_op jit(solution)/shard_map/triangular_solve | solution.py:23
  142.0 1.5 convolution_subtract_fusion.1
  144.0 1.9 convolution_subtract_fusion
  146.4 2.4 convolution_subtract_fusion.2
  152.9 51.2 %all-gather.3.cloned.1.call-done = f32[4,512,512]{2,1,0:T(8,128)} async-done(((f32[1,512,512]{2,1,0:T(8,128)}), f32[4,512,512]{2,1,0:T(8,128)}) %all-gather.3.cloned.1.call-update) | async-done | bytes 4194320 | tf_op jit(solution)/shard_map/all_gather | solution.py:10
  204.1 2.8 reduce_sum.19
  206.9 50.3 %all-gather.5.cloned.1.call-done = f32[2048,512]{0,1:T(8,128)} async-done(((f32[512,512]{0,1:T(8,128)}), f32[2048,512]{0,1:T(8,128)}) %all-gather.5.cloned.1.call-update) | async-done | bytes 4194320 | tf_op jit(solution)/shard_map/all_gather | solution.py:29
  257.2 9.6 %fusion.1 = f32[64,8,16,128]{3,1,2,0:T(8,128)S(1)} fusion(f32[1,512,2048]{2,1,0:T(8,128)} %param.9, f32[512,512]{1,0:T(8,128)S(1)} %reduce_sum.19, f32[2048,512]{0,1:T(8,128)} %all-gather.5.cloned.1.call-done, pred[2048]{0:T(1024)(128)(4,1)S(1)} %add_compare_fusion), kind=kOutput, calls=%fused_computation.5 | convolution fusion | flops 6444548096 | bytes 13633536 | tf_op jit(solution)/shard_map/dot_general | solution.py:27
  268.2 3.3 copy.19
  271.4 4.9 reshape.201
  276.4 8.7 %fusion.33 = f32[16,8,16384]{2,1,0:T(8,128)} fusion(f32[64,16384,1]{1,0,2:T(8,128)} %reshape.201, s32[16,8]{1,0:T(8,128)S(1)} %multiply_add_fusion, s32[64]{0:T(128)S(1)} %multiply_add_fusion.1), kind=kOutput, calls=%fused_computation.67 | convolution fusion | flops 1610620928 | bytes 12583680 | tf_op jit(solution)/shard_map/dot_general | solution.py:65
  285.1 9.7 %all-to-all-start = ((f32[16,8,16384]{2,1,0:T(8,128)}), f32[16,8,16384]{2,1,0:T(8,128)}, u32[]{:S(2)}, u32[]{:S(2)}) async-start(f32[16,8,16384]{2,1,0:T(8,128)} %fusion.33), calls=%async_computation | async-start | bytes 16777216 | tf_op jit(solution)/shard_map/all_to_all | solution.py:66
  295.3 192.4 %all-to-all-done = f32[16,8,16384]{2,1,0:T(8,128)} async-done(((f32[16,8,16384]{2,1,0:T(8,128)}), f32[16,8,16384]{2,1,0:T(8,128)}, u32[]{:S(2)}, u32[]{:S(2)}) %all-to-all-start) | async-done | bytes 8388640 | tf_op jit(solution)/shard_map/all_to_all | solution.py:66
  487.7 9.0 %copy.20 = f32[16384,128]{1,0:T(8,128)} copy(f32[16384,128]{0,1:T(8,128)} %bitcast.30) | data formatting | bytes 16777216 | tf_op jit(solution)/shard_map/dot_general | solution.py:77
  496.7 9.4 %convolution_bitcast_fusion = f32[1,128,16,128]{3,2,1,0:T(8,128)S(1)} fusion(f32[16,128,1]{0,1,2:T(8,128)S(1)} %convolution_bitcast_fusion.1, f32[128,128,128]{2,1,0:T(8,128)} %bitcast.108), kind=kOutput, calls=%fused_computation.6 | convolution fusion | flops 402653184 | bytes 9445376 | tf_op jit(solution)/shard_map/dot_general | solution.py:77
  (66 shorter events, 22.4 us)
Async XLA Ops:
  6.5 197.6 %all-gather.3.cloned.1.call-start = ((), (), s32[]{:S(2)}) async-start(), calls=%async_computation.1 | async-start | bytes 5242880 | tf_op jit(solution)/shard_map/all_gather | solution.py:10
  149.2 3.3 copy-start.1
  150.6 106.6 %all-gather.5.cloned.1.call-start = ((), (), s32[]{:S(2)}) async-start(), calls=%async_computation.2 | async-start | bytes 5242880 | tf_op jit(solution)/shard_map/all_gather | solution.py:29
  285.1 10.0 %copy-start.2 = (s32[16,1,1,64,1]{3,4,2,1,0:T(1,128)S(1)}, s32[16,1,1,64,1]{3,4,2,1,0:T(1,128)}, u32[]{:S(2)}) copy-start(s32[16,1,1,64,1]{3,4,2,1,0:T(1,128)} %param.13) | copy-start | bytes 12292
  285.1 202.6 %all-to-all-start = ((f32[16,8,16384]{2,1,0:T(8,128)}), f32[16,8,16384]{2,1,0:T(8,128)}, u32[]{:S(2)}, u32[]{:S(2)}) async-start(f32[16,8,16384]{2,1,0:T(8,128)} %fusion.33), calls=%async_computation | async-start | bytes 16777216 | tf_op jit(solution)/shard_map/all_to_all | solution.py:66
  496.7 9.6 %copy-start = (f32[1,128,2048]{2,1,0:T(8,128)S(1)}, f32[1,128,2048]{2,1,0:T(8,128)}, u32[]{:S(2)}) copy-start(f32[1,128,2048]{2,1,0:T(8,128)} %param.10) | copy-start | bytes 3145732
Sparse Core Ops, SparseCore 0:
  150.8 53.3 all-gather.2
  205.9 51.2 all-gather.4
